TPU v7x, 128 devices: a whole 4x4x4 slice. The times are simulated.
128 devices in a mesh: row: 16 (over y, x), col: 8 (over z, core).
Axes of the slice: x: 4, y: 4, z: 4, core: 2. Of those that a mesh axis runs over, the one named last changes fastest.
Arguments:
- front_first: float32 [16, 4, 128, 8, 8, 128], P('row', None, None, 'col'), as said below
- front_second: float32 [16, 4, 128, 8, 8, 128], P('row', None, None, 'col'), as said below
- front_third: float32 [16, 4, 128, 8, 8, 128], P('row', None, None, 'col'), as said below
- map_second: int32 [60], replicated, may hold values from 0 to 63, as said below
- map_third: int32 [60], replicated, may hold values from 0 to 63, as said below
Outputs:
- lower_first: float32 [16, 4, 128, 512], P('row')
- lower_second: float32 [16, 4, 128, 512], P('row')
- lower_third: float32 [16, 4, 128, 512], P('row')
- schur_third: float32 [16, 4, 128, 8, 8, 128], P('row', None, None, 'col')
Inputs may be any that keep to these rules, and one draw needn't show every extreme that they name: `map_second`: strictly increasing; the first entry is 0 and the last is 63. `map_third`: strictly increasing; the first entry is 0 and the last is 63. `front_first`: symmetric positive definite. `front_second`: symmetric positive definite. `front_third`: symmetric positive definite.
All inputs are finite; a program needn't handle non-finite values.
Results may differ from a plain program's by a relative error of at most 0.00012.
Values sent between devices are 32-bit elements; how exact they have to be, the bound alone decides.
No kernel may reach another device: no remote copies, remote signals or barrier semaphores. Data moves between devices by JAX's collectives and lax.ppermute only.
A program may use at most 128 MiB of HBM per device.

v0:
```python
import jax
import jax.numpy as jnp
from jax import lax
from jax.sharding import PartitionSpec as P

TILE = 128
PANEL = 512
PIVOTS = 512


def shifted(value, axis, steps):
    count = lax.axis_size(axis)
    pairs = [(source, (source + steps) % count) for source in range(count)]
    return lax.ppermute(value, axis, pairs)


def spread(block, axis, source):
    block = jnp.where(lax.axis_index(axis) == source, block, jnp.zeros_like(block))
    return lax.psum(block, axis)


def shift_rows(block_data, amount):
    return shifted(block_data, "row", amount)


def shift_cols(block_data, amount):
    return shifted(block_data, "col", amount)


def relocate(block_data, block_map, axis_dim, count, index, shifter):
    pivot_blocks = PIVOTS // TILE
    local_tiles = block_data.shape[axis_dim]
    child_start = jnp.arange(block_map.shape[0], dtype=jnp.int32) + pivot_blocks
    displacement = child_start - block_map
    local_pos = jnp.arange(local_tiles, dtype=jnp.int32) * count + index
    for bit_index in reversed(range(pivot_blocks.bit_length())):
        stride = 1 << bit_index
        high_part = displacement >> bit_index + 1 << bit_index + 1
        where_now = child_start - high_part
        moving_now = displacement >> bit_index & 1 == 1
        moving = jnp.any((where_now[None, :] == local_pos[:, None]) & moving_now[None, :], axis=1)
        if axis_dim == 0:
            tile_mask = moving[:, None, None, None]
        else:
            tile_mask = moving[None, None, :, None]
        sending = jnp.where(tile_mask, block_data, 0.0)
        staying = jnp.where(tile_mask, 0.0, block_data)
        full_turns = stride // count
        remainder = stride % count
        arrived = shifter(sending, count - remainder)
        roll_amount = full_turns + (index + remainder >= count).astype(jnp.int32)
        arrived = jnp.roll(arrived, -roll_amount, axis=axis_dim)
        block_data = staying + arrived
    return block_data


def per_device(front_first, front_second, front_third, map_second, map_third):
    row_count = lax.axis_size("row")
    col_count = lax.axis_size("col")
    row_index = lax.axis_index("row")
    col_index = lax.axis_index("col")
    tiles_row = front_first.shape[1]
    tile_size = front_first.shape[2]
    tiles_col = front_first.shape[4]
    panel_tiles = PANEL // tile_size
    row_logical = (
        (jnp.arange(tiles_row, dtype=jnp.int32) * row_count + row_index)[:, None] * tile_size
        + jnp.arange(tile_size, dtype=jnp.int32)[None, :]
    ).reshape(-1)
    col_logical = (
        (jnp.arange(tiles_col, dtype=jnp.int32) * col_count + col_index)[:, None] * tile_size
        + jnp.arange(tile_size, dtype=jnp.int32)[None, :]
    ).reshape(-1)

    def local_form(front):
        return front.reshape(tiles_row, tile_size, tiles_col, tile_size)

    def factor_local(matrix):
        first_tile = 0 // tile_size
        pieces = []
        for member in range(panel_tiles):
            global_col = first_tile + member
            pieces.append(
                spread(matrix[:, :, global_col // col_count, :], "col", global_col % col_count)
            )
        panel_cols = jnp.stack(pieces, axis=2).reshape(tiles_row * tile_size, PANEL)
        panel_tiled = panel_cols.reshape(tiles_row, tile_size, PANEL)
        diagonal_parts = []
        for member in range(panel_tiles):
            global_row = first_tile + member
            diagonal_parts.append(
                spread(panel_tiled[global_row // row_count], "row", global_row % row_count)
            )
        diagonal = jnp.concatenate(diagonal_parts, axis=0)
        factor_block = jnp.linalg.cholesky(diagonal)
        inverse = lax.linalg.triangular_solve(
            factor_block, jnp.eye(PANEL, dtype=jnp.float32), left_side=True, lower=True
        )
        lower_panel = jnp.dot(
            panel_cols,
            inverse.T,
            precision=lax.Precision.HIGHEST,
            preferred_element_type=jnp.float32,
        )
        lower_panel = jnp.where((row_logical >= 0)[:, None], lower_panel, 0.0)
        received = []
        for member in range(row_count // col_count):
            got = spread(lower_panel, "row", member * col_count + col_index)
            received.append(got.reshape(tiles_row, tile_size, PANEL))
        column_side = jnp.stack(received, axis=1).reshape(tiles_col * tile_size, PANEL)
        update = jnp.dot(
            lower_panel,
            column_side.T,
            precision=lax.Precision.HIGHEST,
            preferred_element_type=jnp.float32,
        )
        matrix = matrix - update.reshape(tiles_row, tile_size, tiles_col, tile_size)
        row_keep = (row_logical >= PIVOTS).reshape(tiles_row, tile_size)
        col_keep = (col_logical >= PIVOTS).reshape(tiles_col, tile_size)
        schur = jnp.where(row_keep[:, :, None, None] & col_keep[None, None, :, :], matrix, 0.0)
        return (lower_panel, schur)

    def extend_local(parent, schur, block_map):
        moved = relocate(schur, block_map, 0, row_count, row_index, shift_rows)
        moved = relocate(moved, block_map, 2, col_count, col_index, shift_cols)
        return parent + moved

    lower_first, schur_first = factor_local(local_form(front_first))
    lower_second, schur_second = factor_local(
        extend_local(local_form(front_second), schur_first, map_second)
    )
    lower_third, schur_third = factor_local(
        extend_local(local_form(front_third), schur_second, map_third)
    )
    out_shape = (1, tiles_row, tile_size, PIVOTS)
    return (
        lower_first.reshape(out_shape),
        lower_second.reshape(out_shape),
        lower_third.reshape(out_shape),
        schur_third.reshape(1, tiles_row, tile_size, 1, tiles_col, tile_size),
    )


def solution(mesh):
    return jax.shard_map(
        per_device,
        mesh=mesh,
        in_specs=(
            P("row", None, None, "col", None, None),
            P("row", None, None, "col", None, None),
            P("row", None, None, "col", None, None),
            P(),
            P(),
        ),
        out_specs=(
            P("row", None, None, None),
            P("row", None, None, None),
            P("row", None, None, None),
            P("row", None, None, "col", None, None),
        ),
        check_vma=False,
    )
```

profile of v0, /device:TPU:0, one launch (start us, length us, event | category | flops | bytes accessed | tf_op | source)
XLA Modules:
  0.0 1831.1 jit_solution(12885181710065170013)
XLA Ops:
  10.3 66.3 %all-reduce.36.cloned.1.call-done = (f32[4,128,1,128]{3,1,2,0:T(8,128)}, f32[4,128,1,128]{3,1,2,0:T(8,128)}, f32[4,128,1,128]{3,1,2,0:T(8,128)}, f32[4,128,1,128]{3,1,2,0:T(8,128)}) async-done(((f32[4,128,1,128]{3,1,2,0:T(8,128)}, f32[4,128,1,128]{3,1,2,0:T(8,128)}, f32[4,128,1,128]{3,1,2,0:T(8,128)}, f32[4,128,1,128]{3,1,2,0:T(8,128)}), (f32[4,128,1,128]{3,1,2,0:T(8,128)}, f32[4,128,1,128]{3,1,2,0:T(8,128)}, ...) | async-done | bytes 1048592 | tf_op jit(solution)/shard_map/psum | solution.py:19
  85.9 84.5 %all-reduce.30.cloned.1.call-done = (f32[128,512]{0,1:T(8,128)}, f32[128,512]{0,1:T(8,128)}, f32[128,512]{0,1:T(8,128)}, f32[128,512]{0,1:T(8,128)}) async-done(((f32[128,512]{0,1:T(8,128)}, f32[128,512]{0,1:T(8,128)}, f32[128,512]{0,1:T(8,128)}, f32[128,512]{0,1:T(8,128)}), (f32[128,512]{0,1:T(8,128)}, f32[128,512]{0,1:T(8,128)}, f32[128,512]{0,1:T(8,128)}, ...) | async-done | bytes 1048592 | tf_op jit(solution)/shard_map/psum | solution.py:19
  271.2 39.3 %custom-call.34 = f32[4,128,128]{1,2,0:T(8,128)S(1)} custom-call(f32[4,128,128]{2,1,0:T(8,128)S(1)} %get-tuple-element.28), custom_call_target="InvertDiagBlocksLowerTriangular" | custom-call | tf_op jit(solution)/shard_map/triangular_solve/custom-call.3 | solution.py:96
  318.3 88.9 %all-reduce.28.cloned.1.call-done = (f32[4,1,128,512]{3,2,0,1:T(8,128)}, f32[4,1,128,512]{3,2,0,1:T(8,128)}) async-done(((f32[4,1,128,512]{3,2,0,1:T(8,128)}, f32[4,1,128,512]{3,2,0,1:T(8,128)}), (f32[4,1,128,512]{3,2,0,1:T(8,128)}, f32[4,1,128,512]{3,2,0,1:T(8,128)})) %all-reduce.28.cloned.1.call-update) | async-done | bytes 2097168 | tf_op jit(solution)/shard_map/psum | solution.py:19
  418.5 44.2 %collective-permute-done = f32[4,128,8,128]{3,1,2,0:T(8,128)} collective-permute-done((f32[4,128,8,128]{3,1,2,0:T(8,128)}, f32[4,128,8,128]{3,1,2,0:T(8,128)}, u32[]{:S(2)}, u32[]{:S(2)}) %collective-permute-start) | collective-permute-done | bytes 2097184 | tf_op jit(solution)/shard_map/ppermute | solution.py:14
  471.6 42.9 %collective-permute-done.1 = f32[4,128,8,128]{3,1,2,0:T(8,128)S(1)} collective-permute-done((f32[4,128,8,128]{3,1,2,0:T(8,128)}, f32[4,128,8,128]{3,1,2,0:T(8,128)S(1)}, u32[]{:S(2)}, u32[]{:S(2)}) %collective-permute-start.1) | collective-permute-done | bytes 2097184 | tf_op jit(solution)/shard_map/ppermute | solution.py:14
  526.1 41.8 %collective-permute-done.2 = f32[4,128,8,128]{3,1,2,0:T(8,128)} collective-permute-done((f32[4,128,8,128]{3,1,2,0:T(8,128)}, f32[4,128,8,128]{3,1,2,0:T(8,128)}, u32[]{:S(2)}, u32[]{:S(2)}) %collective-permute-start.2) | collective-permute-done | bytes 2097184 | tf_op jit(solution)/shard_map/ppermute | solution.py:14
  575.6 41.9 %collective-permute-done.3 = f32[4,128,8,128]{3,1,2,0:T(8,128)S(1)} collective-permute-done((f32[4,128,8,128]{3,1,2,0:T(8,128)}, f32[4,128,8,128]{3,1,2,0:T(8,128)S(1)}, u32[]{:S(2)}, u32[]{:S(2)}) %collective-permute-start.3) | collective-permute-done | bytes 2097184 | tf_op jit(solution)/shard_map/ppermute | solution.py:14
  626.3 40.2 %collective-permute-done.4 = f32[4,128,8,128]{3,1,2,0:T(8,128)} collective-permute-done((f32[4,128,8,128]{3,1,2,0:T(8,128)}, f32[4,128,8,128]{3,1,2,0:T(8,128)}, u32[]{:S(2)}, u32[]{:S(2)}) %collective-permute-start.4) | collective-permute-done | bytes 2097184 | tf_op jit(solution)/shard_map/ppermute | solution.py:14
  671.0 23.9 %collective-permute-done.5 = f32[4,128,8,128]{3,1,2,0:T(8,128)S(1)} collective-permute-done((f32[4,128,8,128]{3,1,2,0:T(8,128)}, f32[4,128,8,128]{3,1,2,0:T(8,128)S(1)}, u32[]{:S(2)}, u32[]{:S(2)}) %collective-permute-start.5) | collective-permute-done | bytes 2097184 | tf_op jit(solution)/shard_map/ppermute | solution.py:14
  701.3 66.3 %all-reduce.34.cloned.1.call-done = (f32[4,128,1,128]{3,1,2,0:T(8,128)}, f32[4,128,1,128]{3,1,2,0:T(8,128)}, f32[4,128,1,128]{3,1,2,0:T(8,128)}, f32[4,128,1,128]{3,1,2,0:T(8,128)}) async-done(((f32[4,128,1,128]{3,1,2,0:T(8,128)}, f32[4,128,1,128]{3,1,2,0:T(8,128)}, f32[4,128,1,128]{3,1,2,0:T(8,128)}, f32[4,128,1,128]{3,1,2,0:T(8,128)}), (f32[4,128,1,128]{3,1,2,0:T(8,128)}, f32[4,128,1,128]{3,1,2,0:T(8,128)}, ...) | async-done | bytes 1048592 | tf_op jit(solution)/shard_map/psum | solution.py:19
  782.7 83.4 %all-reduce.26.cloned.1.call-done = (f32[128,512]{0,1:T(8,128)}, f32[128,512]{0,1:T(8,128)}, f32[128,512]{0,1:T(8,128)}, f32[128,512]{0,1:T(8,128)}) async-done(((f32[128,512]{0,1:T(8,128)}, f32[128,512]{0,1:T(8,128)}, f32[128,512]{0,1:T(8,128)}, f32[128,512]{0,1:T(8,128)}), (f32[128,512]{0,1:T(8,128)}, f32[128,512]{0,1:T(8,128)}, f32[128,512]{0,1:T(8,128)}, ...) | async-done | bytes 1048592 | tf_op jit(solution)/shard_map/psum | solution.py:19
  986.0 40.1 %custom-call.38 = f32[4,128,128]{1,2,0:T(8,128)S(1)} custom-call(f32[4,128,128]{2,1,0:T(8,128)} %copy-done.17), custom_call_target="InvertDiagBlocksLowerTriangular" | custom-call | tf_op jit(solution)/shard_map/triangular_solve/custom-call.3 | solution.py:96
  1035.8 89.6 %all-reduce.24.cloned.1.call-done = (f32[4,1,128,512]{3,2,0,1:T(8,128)}, f32[4,1,128,512]{3,2,0,1:T(8,128)}) async-done(((f32[4,1,128,512]{3,2,0,1:T(8,128)}, f32[4,1,128,512]{3,2,0,1:T(8,128)}), (f32[4,1,128,512]{3,2,0,1:T(8,128)}, f32[4,1,128,512]{3,2,0,1:T(8,128)})) %all-reduce.24.cloned.1.call-update) | async-done | bytes 2097168 | tf_op jit(solution)/shard_map/psum | solution.py:19
  1134.6 43.9 %collective-permute-done.6 = f32[4,128,8,128]{3,1,2,0:T(8,128)S(1)} collective-permute-done((f32[4,128,8,128]{3,1,2,0:T(8,128)S(1)}, f32[4,128,8,128]{3,1,2,0:T(8,128)S(1)}, u32[]{:S(2)}, u32[]{:S(2)}) %collective-permute-start.6) | collective-permute-done | bytes 2097184 | tf_op jit(solution)/shard_map/ppermute | solution.py:14
  1183.9 42.6 %collective-permute-done.7 = f32[4,128,8,128]{3,1,2,0:T(8,128)S(1)} collective-permute-done((f32[4,128,8,128]{3,1,2,0:T(8,128)S(1)}, f32[4,128,8,128]{3,1,2,0:T(8,128)S(1)}, u32[]{:S(2)}, u32[]{:S(2)}) %collective-permute-start.7) | collective-permute-done | bytes 2097184 | tf_op jit(solution)/shard_map/ppermute | solution.py:14
  1233.9 41.2 %collective-permute-done.8 = f32[4,128,8,128]{3,1,2,0:T(8,128)S(1)} collective-permute-done((f32[4,128,8,128]{3,1,2,0:T(8,128)S(1)}, f32[4,128,8,128]{3,1,2,0:T(8,128)S(1)}, u32[]{:S(2)}, u32[]{:S(2)}) %collective-permute-start.8) | collective-permute-done | bytes 2097184 | tf_op jit(solution)/shard_map/ppermute | solution.py:14
  1279.2 41.1 %collective-permute-done.9 = f32[4,128,8,128]{3,1,2,0:T(8,128)S(1)} collective-permute-done((f32[4,128,8,128]{3,1,2,0:T(8,128)S(1)}, f32[4,128,8,128]{3,1,2,0:T(8,128)S(1)}, u32[]{:S(2)}, u32[]{:S(2)}) %collective-permute-start.9) | collective-permute-done | bytes 2097184 | tf_op jit(solution)/shard_map/ppermute | solution.py:14
  1326.6 38.9 %collective-permute-done.10 = f32[4,128,8,128]{3,1,2,0:T(8,128)S(1)} collective-permute-done((f32[4,128,8,128]{3,1,2,0:T(8,128)S(1)}, f32[4,128,8,128]{3,1,2,0:T(8,128)S(1)}, u32[]{:S(2)}, u32[]{:S(2)}) %collective-permute-start.10) | collective-permute-done | bytes 2097184 | tf_op jit(solution)/shard_map/ppermute | solution.py:14
  1366.5 23.5 %collective-permute-done.11 = f32[4,128,8,128]{3,1,2,0:T(8,128)S(1)} collective-permute-done((f32[4,128,8,128]{3,1,2,0:T(8,128)S(1)}, f32[4,128,8,128]{3,1,2,0:T(8,128)S(1)}, u32[]{:S(2)}, u32[]{:S(2)}) %collective-permute-start.11) | collective-permute-done | bytes 2097184 | tf_op jit(solution)/shard_map/ppermute | solution.py:14
  1392.4 66.3 %all-reduce.32.cloned.1.call-done = (f32[4,128,1,128]{3,1,2,0:T(8,128)}, f32[4,128,1,128]{3,1,2,0:T(8,128)}, f32[4,128,1,128]{3,1,2,0:T(8,128)}, f32[4,128,1,128]{3,1,2,0:T(8,128)}) async-done(((f32[4,128,1,128]{3,1,2,0:T(8,128)}, f32[4,128,1,128]{3,1,2,0:T(8,128)}, f32[4,128,1,128]{3,1,2,0:T(8,128)}, f32[4,128,1,128]{3,1,2,0:T(8,128)}), (f32[4,128,1,128]{3,1,2,0:T(8,128)}, f32[4,128,1,128]{3,1,2,0:T(8,128)}, ...) | async-done | bytes 1048592 | tf_op jit(solution)/shard_map/psum | solution.py:19
  1473.8 83.3 %all-reduce.22.cloned.1.call-done = (f32[128,512]{0,1:T(8,128)}, f32[128,512]{0,1:T(8,128)}, f32[128,512]{0,1:T(8,128)}, f32[128,512]{0,1:T(8,128)}) async-done(((f32[128,512]{0,1:T(8,128)}, f32[128,512]{0,1:T(8,128)}, f32[128,512]{0,1:T(8,128)}, f32[128,512]{0,1:T(8,128)}), (f32[128,512]{0,1:T(8,128)}, f32[128,512]{0,1:T(8,128)}, f32[128,512]{0,1:T(8,128)}, ...) | async-done | bytes 1048592 | tf_op jit(solution)/shard_map/psum | solution.py:19
  1677.1 40.1 %custom-call.42 = f32[4,128,128]{1,2,0:T(8,128)S(1)} custom-call(f32[4,128,128]{2,1,0:T(8,128)} %copy-done.16), custom_call_target="InvertDiagBlocksLowerTriangular" | custom-call | tf_op jit(solution)/shard_map/triangular_solve/custom-call.3 | solution.py:96
  1726.4 89.9 %all-reduce.20.cloned.1.call-done = (f32[4,1,128,512]{3,2,0,1:T(8,128)}, f32[4,1,128,512]{3,2,0,1:T(8,128)}) async-done(((f32[4,1,128,512]{3,2,0,1:T(8,128)}, f32[4,1,128,512]{3,2,0,1:T(8,128)}), (f32[4,1,128,512]{3,2,0,1:T(8,128)}, f32[4,1,128,512]{3,2,0,1:T(8,128)})) %all-reduce.20.cloned.1.call-update) | async-done | bytes 2097168 | tf_op jit(solution)/shard_map/psum | solution.py:19
  (298 shorter events, 536.3 us)
Async XLA Ops:
  7.2 69.4 %all-reduce.36.cloned.1.call-start = ((), (), s32[]{:S(2)}) async-start(), calls=%async_computation.8 | async-start | bytes 2097152 | tf_op jit(solution)/shard_map/psum | solution.py:19
  10.2 160.2 %all-reduce.30.cloned.1.call-start = ((), (), s32[]{:S(2)}) async-start(), calls=%async_computation.5 | async-start | bytes 2097152 | tf_op jit(solution)/shard_map/psum | solution.py:19
  84.0 323.2 %all-reduce.28.cloned.1.call-start = ((), (), s32[]{:S(2)}) async-start(), calls=%async_computation.4 | async-start | bytes 4194304 | tf_op jit(solution)/shard_map/psum | solution.py:19
  317.3 450.3 %all-reduce.34.cloned.1.call-start = ((), (), s32[]{:S(2)}) async-start(), calls=%async_computation.7 | async-start | bytes 2097152 | tf_op jit(solution)/shard_map/psum | solution.py:19
  416.1 46.6 %collective-permute-start = (f32[4,128,8,128]{3,1,2,0:T(8,128)}, f32[4,128,8,128]{3,1,2,0:T(8,128)}, u32[]{:S(2)}, u32[]{:S(2)}) collective-permute-start(f32[4,128,8,128]{3,1,2,0:T(8,128)} %get-tuple-element.212), channel_id=1, source_target_pairs={{0,96},{8,104},{16,112},{24,120},{32,0},{40,8},{48,16},{56,24},{64... | collective-permute-start | bytes 6291464 | tf_op jit(solution)/shard_map/ppermute | solution.py:14
  467.2 47.2 %collective-permute-start.1 = (f32[4,128,8,128]{3,1,2,0:T(8,128)}, f32[4,128,8,128]{3,1,2,0:T(8,128)S(1)}, u32[]{:S(2)}, u32[]{:S(2)}) collective-permute-start(f32[4,128,8,128]{3,1,2,0:T(8,128)} %get-tuple-element.127), channel_id=1, source_target_pairs={{0,112},{8,120},{16,0},{24,8},{32,16},{40,24},{48,32},{56,40},{64,... | collective-permute-start | bytes 6291464 | tf_op jit(solution)/shard_map/ppermute | solution.py:14
  520.2 47.8 %collective-permute-start.2 = (f32[4,128,8,128]{3,1,2,0:T(8,128)}, f32[4,128,8,128]{3,1,2,0:T(8,128)}, u32[]{:S(2)}, u32[]{:S(2)}) collective-permute-start(f32[4,128,8,128]{3,1,2,0:T(8,128)} %get-tuple-element.125), channel_id=1, source_target_pairs={{0,120},{8,0},{16,8},{24,16},{32,24},{40,32},{48,40},{56,48},{64,5... | collective-permute-start | bytes 6291464 | tf_op jit(solution)/shard_map/ppermute | solution.py:14
  572.4 45.0 %collective-permute-start.3 = (f32[4,128,8,128]{3,1,2,0:T(8,128)}, f32[4,128,8,128]{3,1,2,0:T(8,128)S(1)}, u32[]{:S(2)}, u32[]{:S(2)}) collective-permute-start(f32[4,128,8,128]{3,1,2,0:T(8,128)} %get-tuple-element.123), channel_id=1, source_target_pairs={{0,4},{1,5},{2,6},{3,7},{4,0},{5,1},{6,2},{7,3},{8,12},{9,13},{10,... | collective-permute-start | bytes 6291464 | tf_op jit(solution)/shard_map/ppermute | solution.py:14
  623.3 43.2 %collective-permute-start.4 = (f32[4,128,8,128]{3,1,2,0:T(8,128)}, f32[4,128,8,128]{3,1,2,0:T(8,128)}, u32[]{:S(2)}, u32[]{:S(2)}) collective-permute-start(f32[4,128,8,128]{3,1,2,0:T(8,128)} %get-tuple-element.121), channel_id=1, source_target_pairs={{0,6},{1,7},{2,0},{3,1},{4,2},{5,3},{6,4},{7,5},{8,14},{9,15},{10,... | collective-permute-start | bytes 6291464 | tf_op jit(solution)/shard_map/ppermute | solution.py:14
  671.0 23.9 %collective-permute-start.5 = (f32[4,128,8,128]{3,1,2,0:T(8,128)}, f32[4,128,8,128]{3,1,2,0:T(8,128)S(1)}, u32[]{:S(2)}, u32[]{:S(2)}) collective-permute-start(f32[4,128,8,128]{3,1,2,0:T(8,128)} %get-tuple-element.119), channel_id=1, source_target_pairs={{0,7},{1,0},{2,1},{3,2},{4,3},{5,4},{6,5},{7,6},{8,15},{9,8},{10,9... | collective-permute-start | bytes 6291464 | tf_op jit(solution)/shard_map/ppermute | solution.py:14
  701.3 164.8 %all-reduce.26.cloned.1.call-start = ((), (), s32[]{:S(2)}) async-start(), calls=%async_computation.3 | async-start | bytes 2097152 | tf_op jit(solution)/shard_map/psum | solution.py:19
  779.6 345.9 %all-reduce.24.cloned.1.call-start = ((), (), s32[]{:S(2)}) async-start(), calls=%async_computation.2 | async-start | bytes 4194304 | tf_op jit(solution)/shard_map/psum | solution.py:19
  1027.8 4.2 copy-start.5
  1035.6 423.0 %all-reduce.32.cloned.1.call-start = ((), (), s32[]{:S(2)}) async-start(), calls=%async_computation.6 | async-start | bytes 2097152 | tf_op jit(solution)/shard_map/psum | solution.py:19
  1132.2 46.3 %collective-permute-start.6 = (f32[4,128,8,128]{3,1,2,0:T(8,128)S(1)}, f32[4,128,8,128]{3,1,2,0:T(8,128)S(1)}, u32[]{:S(2)}, u32[]{:S(2)}) collective-permute-start(f32[4,128,8,128]{3,1,2,0:T(8,128)S(1)} %get-tuple-element.217), channel_id=1, source_target_pairs={{0,96},{8,104},{16,112},{24,120},{32,0},{40,8},{48,16},{56,24},{64... | collective-permute-start | bytes 6291464 | tf_op jit(solution)/shard_map/ppermute | solution.py:14
  1179.4 47.0 %collective-permute-start.7 = (f32[4,128,8,128]{3,1,2,0:T(8,128)S(1)}, f32[4,128,8,128]{3,1,2,0:T(8,128)S(1)}, u32[]{:S(2)}, u32[]{:S(2)}) collective-permute-start(f32[4,128,8,128]{3,1,2,0:T(8,128)S(1)} %get-tuple-element.117), channel_id=1, source_target_pairs={{0,112},{8,120},{16,0},{24,8},{32,16},{40,24},{48,32},{56,40},{64,... | collective-permute-start | bytes 6291464 | tf_op jit(solution)/shard_map/ppermute | solution.py:14
  1227.4 47.6 %collective-permute-start.8 = (f32[4,128,8,128]{3,1,2,0:T(8,128)S(1)}, f32[4,128,8,128]{3,1,2,0:T(8,128)S(1)}, u32[]{:S(2)}, u32[]{:S(2)}) collective-permute-start(f32[4,128,8,128]{3,1,2,0:T(8,128)S(1)} %get-tuple-element.115), channel_id=1, source_target_pairs={{0,120},{8,0},{16,8},{24,16},{32,24},{40,32},{48,40},{56,48},{64,5... | collective-permute-start | bytes 6291464 | tf_op jit(solution)/shard_map/ppermute | solution.py:14
  1276.0 44.3 %collective-permute-start.9 = (f32[4,128,8,128]{3,1,2,0:T(8,128)S(1)}, f32[4,128,8,128]{3,1,2,0:T(8,128)S(1)}, u32[]{:S(2)}, u32[]{:S(2)}) collective-permute-start(f32[4,128,8,128]{3,1,2,0:T(8,128)S(1)} %get-tuple-element.113), channel_id=1, source_target_pairs={{0,4},{1,5},{2,6},{3,7},{4,0},{5,1},{6,2},{7,3},{8,12},{9,13},{10,... | collective-permute-start | bytes 6291464 | tf_op jit(solution)/shard_map/ppermute | solution.py:14
  1321.3 44.3 %collective-permute-start.10 = (f32[4,128,8,128]{3,1,2,0:T(8,128)S(1)}, f32[4,128,8,128]{3,1,2,0:T(8,128)S(1)}, u32[]{:S(2)}, u32[]{:S(2)}) collective-permute-start(f32[4,128,8,128]{3,1,2,0:T(8,128)S(1)} %get-tuple-element.111), channel_id=1, source_target_pairs={{0,6},{1,7},{2,0},{3,1},{4,2},{5,3},{6,4},{7,5},{8,14},{9,15},{10,... | collective-permute-start | bytes 6291464 | tf_op jit(solution)/shard_map/ppermute | solution.py:14
  1365.5 24.5 %copy-start.12 = (f32[1,4,128,1,8,128]{5,4,3,2,1,0:T(8,128)S(1)}, f32[1,4,128,1,8,128]{5,4,3,2,1,0:T(8,128)}, u32[]{:S(2)}) copy-start(f32[1,4,128,1,8,128]{5,4,3,2,1,0:T(8,128)} %param.14) | copy-start | bytes 6291460
  1366.5 23.6 %collective-permute-start.11 = (f32[4,128,8,128]{3,1,2,0:T(8,128)S(1)}, f32[4,128,8,128]{3,1,2,0:T(8,128)S(1)}, u32[]{:S(2)}, u32[]{:S(2)}) collective-permute-start(f32[4,128,8,128]{3,1,2,0:T(8,128)S(1)} %get-tuple-element.109), channel_id=1, source_target_pairs={{0,7},{1,0},{2,1},{3,2},{4,3},{5,4},{6,5},{7,6},{8,15},{9,8},{10,9... | collective-permute-start | bytes 6291464 | tf_op jit(solution)/shard_map/ppermute | solution.py:14
  1392.3 164.8 %all-reduce.22.cloned.1.call-start = ((), (), s32[]{:S(2)}) async-start(), calls=%async_computation.1 | async-start | bytes 2097152 | tf_op jit(solution)/shard_map/psum | solution.py:19
  1470.7 345.6 %all-reduce.20.cloned.1.call-start = ((), (), s32[]{:S(2)}) async-start(), calls=%async_computation | async-start | bytes 4194304 | tf_op jit(solution)/shard_map/psum | solution.py:19
  1726.3 91.8 %copy-start.6 = (f32[512,512]{1,0:T(8,128)}, f32[512,512]{1,0:T(8,128)S(1)}, u32[]{:S(2)}) copy-start(f32[512,512]{1,0:T(8,128)S(1)} %get-tuple-element.221) | copy-start | bytes 3145732
  (17 other events, 22.8 us)
Sparse Core Ops, SparseCore 0:
  11.2 65.3 all-reduce.35
  84.1 86.3 all-reduce.29
  317.4 89.6 all-reduce.27
  701.4 66.1 all-reduce.33
  779.7 86.3 all-reduce.25
  1035.7 89.6 all-reduce.23
  1392.4 66.1 all-reduce.31
  1470.8 86.3 all-reduce.21
  1726.5 89.7 all-reduce.19
where the time goes:
time: 1840 us; the launch traced here: 1830 us
  waiting for transfers between devices  1180 us (64%)
  other arithmetic  413 us (22%)
  local copies, waits for them, and re-layouts  110 us (6%)
  matrix products  58.9 us (3%)
  starting transfers between devices  41.9 us (2%)
  between operations  22.7 us (1%)
    psum x9, waiting for transfers between devices, spread(): return lax.psum(block, axis)  718 us
    ppermute x12, waiting for transfers between devices, shifted(): return lax.ppermute(value, axis, pairs)  466 us
    another operation x44, other arithmetic, factor_local(): factor_block = jnp.linalg.cholesky(diagonal)  242 us
    another operation x7, other arithmetic, factor_local(): lax.linalg.triangular_solve(factor_block, jnp.eye(PANEL, dtype=jnp.float3...  124 us
    ppermute x12, starting transfers between devices, shifted(): return lax.ppermute(value, axis, pairs)  40.5 us
    unnamed x60, local copies, waits for them, and re-layouts  39.2 us
  transfers between devices with their start and end apart: 21, of which 21 were waited for; matrix products, arithmetic and copies ran while one was open for 0% of the time, Pallas kernels for 0%

commit v1 on v0

--- a/solution.py
+++ b/solution.py
@@ -16,7 +16,7 @@
 
 def spread(block, axis, source):
     block = jnp.where(lax.axis_index(axis) == source, block, jnp.zeros_like(block))
-    return lax.psum(block, axis)
+    return jnp.sum(lax.all_gather(block, axis), axis=0)
 
 
 def shift_rows(block_data, amount):

time: 1840 us -> 2780 us (1.51)
  waiting for transfers between devices: 1180 us -> 2010 us
  other arithmetic: 413 us -> 531 us
    all_gather x0 -> x30, waiting for transfers between devices: none -> 1530 us  [spread(): return jnp.sum(lax.all_gather(block, axis), axis=0)]
    psum x9 -> x0, waiting for transfers between devices: 718 us -> none  [spread(): return lax.psum(block, axis)]
    reduce_sum x0 -> x30, other arithmetic: none -> 112 us  [spread(): return jnp.sum(lax.all_gather(block, axis), axis=0)]
  transfers between devices with their start and end apart: 21 -> 42, of which waited for: 21 -> 42; matrix products, arithmetic and copies ran while one was open for 0% -> 4% of each run, Pallas kernels for 0% -> 0%
where the time goes in v1:
time: 2780 us; the launch traced here: 2770 us
  waiting for transfers between devices  2010 us (72%)
  other arithmetic  531 us (19%)
  local copies, waits for them, and re-layouts  106 us (4%)
  matrix products  55.6 us (2%)
  starting transfers between devices  41.4 us (1%)
    all_gather x30, waiting for transfers between devices, spread(): return jnp.sum(lax.all_gather(block, axis), axis=0)  1530 us
    ppermute x12, waiting for transfers between devices, shifted(): return lax.ppermute(value, axis, pairs)  481 us
    another operation x44, other arithmetic, factor_local(): factor_block = jnp.linalg.cholesky(diagonal)  242 us
    another operation x7, other arithmetic, factor_local(): lax.linalg.triangular_solve(factor_block, jnp.eye(PANEL, dtype=jnp.float3...  124 us
    reduce_sum x30, other arithmetic, spread(): return jnp.sum(lax.all_gather(block, axis), axis=0)  112 us
  transfers between devices with their start and end apart: 42, of which 42 were waited for; matrix products, arithmetic and copies ran while one was open for 4% of the time, Pallas kernels for 0%

profile of v1, /device:TPU:0, one launch (start us, length us, event | category | flops | bytes accessed | tf_op | source)
XLA Modules:
  0.0 2772.4 jit_solution(99220049436442272)
XLA Ops:
  130.8 46.3 %all-gather.55.cloned.1.call-done = f32[16,128,512]{2,1,0:T(8,128)} async-done(((f32[1,128,512]{2,1,0:T(8,128)}), f32[16,128,512]{2,1,0:T(8,128)}) %all-gather.55.cloned.1.call-update) | async-done | bytes 4194320 | tf_op jit(solution)/shard_map/all_gather | solution.py:19
  179.9 50.9 %all-gather.53.cloned.1.call-done = f32[16,128,512]{2,1,0:T(8,128)} async-done(((f32[1,128,512]{2,1,0:T(8,128)}), f32[16,128,512]{2,1,0:T(8,128)}) %all-gather.53.cloned.1.call-update) | async-done | bytes 4194320 | tf_op jit(solution)/shard_map/all_gather | solution.py:19
  233.6 51.1 %all-gather.51.cloned.1.call-done = f32[16,128,512]{2,1,0:T(8,128)} async-done(((f32[1,128,512]{2,1,0:T(8,128)}), f32[16,128,512]{2,1,0:T(8,128)}) %all-gather.51.cloned.1.call-update) | async-done | bytes 4194320 | tf_op jit(solution)/shard_map/all_gather | solution.py:19
  287.5 50.5 %all-gather.49.cloned.1.call-done = f32[16,128,512]{2,1,0:T(8,128)} async-done(((f32[1,128,512]{2,1,0:T(8,128)}), f32[16,128,512]{2,1,0:T(8,128)}) %all-gather.49.cloned.1.call-update) | async-done | bytes 4194320 | tf_op jit(solution)/shard_map/all_gather | solution.py:19
  482.4 109.6 %all-gather.83.cloned.1.call-done = f32[8192,512]{1,0:T(8,128)} async-done(((f32[512,512]{1,0:T(8,128)}), f32[8192,512]{1,0:T(8,128)}) %all-gather.83.cloned.1.call-update) | async-done | bytes 16777232 | tf_op jit(solution)/shard_map/all_gather | solution.py:19
  599.9 105.6 %all-gather.81.cloned.1.call-done = f32[8192,512]{1,0:T(8,128)} async-done(((f32[512,512]{1,0:T(8,128)}), f32[8192,512]{1,0:T(8,128)}) %all-gather.81.cloned.1.call-update) | async-done | bytes 16777232 | tf_op jit(solution)/shard_map/all_gather | solution.py:19
  723.3 45.2 %collective-permute-done = f32[4,128,8,128]{3,1,2,0:T(8,128)} collective-permute-done((f32[4,128,8,128]{3,1,2,0:T(8,128)}, f32[4,128,8,128]{3,1,2,0:T(8,128)}, u32[]{:S(2)}, u32[]{:S(2)}) %collective-permute-start) | collective-permute-done | bytes 2097184 | tf_op jit(solution)/shard_map/ppermute | solution.py:14
  777.5 44.3 %collective-permute-done.1 = f32[4,128,8,128]{3,1,2,0:T(8,128)S(1)} collective-permute-done((f32[4,128,8,128]{3,1,2,0:T(8,128)}, f32[4,128,8,128]{3,1,2,0:T(8,128)S(1)}, u32[]{:S(2)}, u32[]{:S(2)}) %collective-permute-start.1) | collective-permute-done | bytes 2097184 | tf_op jit(solution)/shard_map/ppermute | solution.py:14
  833.4 43.2 %collective-permute-done.2 = f32[4,128,8,128]{3,1,2,0:T(8,128)} collective-permute-done((f32[4,128,8,128]{3,1,2,0:T(8,128)}, f32[4,128,8,128]{3,1,2,0:T(8,128)}, u32[]{:S(2)}, u32[]{:S(2)}) %collective-permute-start.2) | collective-permute-done | bytes 2097184 | tf_op jit(solution)/shard_map/ppermute | solution.py:14
  884.2 43.2 %collective-permute-done.3 = f32[4,128,8,128]{3,1,2,0:T(8,128)S(1)} collective-permute-done((f32[4,128,8,128]{3,1,2,0:T(8,128)}, f32[4,128,8,128]{3,1,2,0:T(8,128)S(1)}, u32[]{:S(2)}, u32[]{:S(2)}) %collective-permute-start.3) | collective-permute-done | bytes 2097184 | tf_op jit(solution)/shard_map/ppermute | solution.py:14
  1190.7 48.7 %all-gather.61.cloned.1.call-done = f32[16,128,512]{2,1,0:T(8,128)} async-done(((f32[1,128,512]{2,1,0:T(8,128)}), f32[16,128,512]{2,1,0:T(8,128)}) %all-gather.61.cloned.1.call-update) | async-done | bytes 4194320 | tf_op jit(solution)/shard_map/all_gather | solution.py:19
  1244.5 48.6 %all-gather.59.cloned.1.call-done = f32[16,128,512]{2,1,0:T(8,128)} async-done(((f32[1,128,512]{2,1,0:T(8,128)}), f32[16,128,512]{2,1,0:T(8,128)}) %all-gather.59.cloned.1.call-update) | async-done | bytes 4194320 | tf_op jit(solution)/shard_map/all_gather | solution.py:19
  1298.3 48.0 %all-gather.57.cloned.1.call-done = f32[16,128,512]{2,1,0:T(8,128)} async-done(((f32[1,128,512]{2,1,0:T(8,128)}), f32[16,128,512]{2,1,0:T(8,128)}) %all-gather.57.cloned.1.call-update) | async-done | bytes 4194320 | tf_op jit(solution)/shard_map/all_gather | solution.py:19
  1517.0 110.0 %all-gather.95.cloned.1.call-done = f32[8192,512]{1,0:T(8,128)} async-done(((f32[512,512]{1,0:T(8,128)}), f32[8192,512]{1,0:T(8,128)}) %all-gather.95.cloned.1.call-update) | async-done | bytes 16777232 | tf_op jit(solution)/shard_map/all_gather | solution.py:19
  1635.9 104.6 %all-gather.93.cloned.1.call-done = f32[8192,512]{1,0:T(8,128)} async-done(((f32[512,512]{1,0:T(8,128)}), f32[8192,512]{1,0:T(8,128)}) %all-gather.93.cloned.1.call-update) | async-done | bytes 16777232 | tf_op jit(solution)/shard_map/all_gather | solution.py:19
  1757.8 44.9 %collective-permute-done.6 = f32[4,128,8,128]{3,1,2,0:T(8,128)S(1)} collective-permute-done((f32[4,128,8,128]{3,1,2,0:T(8,128)S(1)}, f32[4,128,8,128]{3,1,2,0:T(8,128)S(1)}, u32[]{:S(2)}, u32[]{:S(2)}) %collective-permute-start.6) | collective-permute-done | bytes 2097184 | tf_op jit(solution)/shard_map/ppermute | solution.py:14
  1808.3 44.0 %collective-permute-done.7 = f32[4,128,8,128]{3,1,2,0:T(8,128)S(1)} collective-permute-done((f32[4,128,8,128]{3,1,2,0:T(8,128)S(1)}, f32[4,128,8,128]{3,1,2,0:T(8,128)S(1)}, u32[]{:S(2)}, u32[]{:S(2)}) %collective-permute-start.7) | collective-permute-done | bytes 2097184 | tf_op jit(solution)/shard_map/ppermute | solution.py:14
  1858.9 43.1 %collective-permute-done.8 = f32[4,128,8,128]{3,1,2,0:T(8,128)S(1)} collective-permute-done((f32[4,128,8,128]{3,1,2,0:T(8,128)S(1)}, f32[4,128,8,128]{3,1,2,0:T(8,128)S(1)}, u32[]{:S(2)}, u32[]{:S(2)}) %collective-permute-start.8) | collective-permute-done | bytes 2097184 | tf_op jit(solution)/shard_map/ppermute | solution.py:14
  1906.2 43.0 %collective-permute-done.9 = f32[4,128,8,128]{3,1,2,0:T(8,128)S(1)} collective-permute-done((f32[4,128,8,128]{3,1,2,0:T(8,128)S(1)}, f32[4,128,8,128]{3,1,2,0:T(8,128)S(1)}, u32[]{:S(2)}, u32[]{:S(2)}) %collective-permute-start.9) | collective-permute-done | bytes 2097184 | tf_op jit(solution)/shard_map/ppermute | solution.py:14
  2199.3 48.7 %all-gather.69.cloned.1.call-done = f32[16,128,512]{2,1,0:T(8,128)} async-done(((f32[1,128,512]{2,1,0:T(8,128)}), f32[16,128,512]{2,1,0:T(8,128)}) %all-gather.69.cloned.1.call-update) | async-done | bytes 4194320 | tf_op jit(solution)/shard_map/all_gather | solution.py:19
  2253.1 48.6 %all-gather.67.cloned.1.call-done = f32[16,128,512]{2,1,0:T(8,128)} async-done(((f32[1,128,512]{2,1,0:T(8,128)}), f32[16,128,512]{2,1,0:T(8,128)}) %all-gather.67.cloned.1.call-update) | async-done | bytes 4194320 | tf_op jit(solution)/shard_map/all_gather | solution.py:19
  2306.8 48.1 %all-gather.65.cloned.1.call-done = f32[16,128,512]{2,1,0:T(8,128)} async-done(((f32[1,128,512]{2,1,0:T(8,128)}), f32[16,128,512]{2,1,0:T(8,128)}) %all-gather.65.cloned.1.call-update) | async-done | bytes 4194320 | tf_op jit(solution)/shard_map/all_gather | solution.py:19
  2524.7 110.5 %all-gather.107.cloned.1.call-done = f32[8192,512]{1,0:T(8,128)} async-done(((f32[512,512]{1,0:T(8,128)}), f32[8192,512]{1,0:T(8,128)}) %all-gather.107.cloned.1.call-update) | async-done | bytes 16777232 | tf_op jit(solution)/shard_map/all_gather | solution.py:19
  2643.1 105.6 %all-gather.105.cloned.1.call-done = f32[8192,512]{1,0:T(8,128)} async-done(((f32[512,512]{1,0:T(8,128)}), f32[8192,512]{1,0:T(8,128)}) %all-gather.105.cloned.1.call-update) | async-done | bytes 16777232 | tf_op jit(solution)/shard_map/all_gather | solution.py:19
  (398 shorter events, 1293.3 us)
Async XLA Ops:
  11.7 110.6 %all-gather.73.cloned.1.call-start = ((), (), s32[]{:S(2)}) async-start(), calls=%async_computation.12 | async-start | bytes 2359296 | tf_op jit(solution)/shard_map/all_gather | solution.py:19
  12.3 164.9 %all-gather.55.cloned.1.call-start = ((), (), s32[]{:S(2)}) async-start(), calls=%async_computation.3 | async-start | bytes 4456448 | tf_op jit(solution)/shard_map/all_gather | solution.py:19
  125.2 105.6 %all-gather.53.cloned.1.call-start = ((), (), s32[]{:S(2)}) async-start(), calls=%async_computation.2 | async-start | bytes 4456448 | tf_op jit(solution)/shard_map/all_gather | solution.py:19
  126.3 158.5 %all-gather.51.cloned.1.call-start = ((), (), s32[]{:S(2)}) async-start(), calls=%async_computation.1 | async-start | bytes 4456448 | tf_op jit(solution)/shard_map/all_gather | solution.py:19
  127.3 210.7 %all-gather.49.cloned.1.call-start = ((), (), s32[]{:S(2)}) async-start(), calls=%async_computation | async-start | bytes 4456448 | tf_op jit(solution)/shard_map/all_gather | solution.py:19
  128.4 463.6 %all-gather.83.cloned.1.call-start = ((), (), s32[]{:S(2)}) async-start(), calls=%async_computation.17 | async-start | bytes 17825792 | tf_op jit(solution)/shard_map/all_gather | solution.py:19
  480.9 224.6 %all-gather.81.cloned.1.call-start = ((), (), s32[]{:S(2)}) async-start(), calls=%async_computation.16 | async-start | bytes 17825792 | tf_op jit(solution)/shard_map/all_gather | solution.py:19
  481.5 559.8 %all-gather.91.cloned.1.call-start = ((), (), s32[]{:S(2)}) async-start(), calls=%async_computation.21 | async-start | bytes 2359296 | tf_op jit(solution)/shard_map/all_gather | solution.py:19
  1013.1 84.3 %all-gather.87.cloned.1.call-start = ((), (), s32[]{:S(2)}) async-start(), calls=%async_computation.19 | async-start | bytes 2359296 | tf_op jit(solution)/shard_map/all_gather | solution.py:19
  1013.9 111.4 %all-gather.85.cloned.1.call-start = ((), (), s32[]{:S(2)}) async-start(), calls=%async_computation.18 | async-start | bytes 2359296 | tf_op jit(solution)/shard_map/all_gather | solution.py:19
  1014.4 171.9 %all-gather.63.cloned.1.call-start = ((), (), s32[]{:S(2)}) async-start(), calls=%async_computation.7 | async-start | bytes 4456448 | tf_op jit(solution)/shard_map/all_gather | solution.py:19
  1134.4 105.1 %all-gather.61.cloned.1.call-start = ((), (), s32[]{:S(2)}) async-start(), calls=%async_computation.6 | async-start | bytes 4456448 | tf_op jit(solution)/shard_map/all_gather | solution.py:19
  1138.0 155.1 %all-gather.59.cloned.1.call-start = ((), (), s32[]{:S(2)}) async-start(), calls=%async_computation.5 | async-start | bytes 4456448 | tf_op jit(solution)/shard_map/all_gather | solution.py:19
  1141.7 204.6 %all-gather.57.cloned.1.call-start = ((), (), s32[]{:S(2)}) async-start(), calls=%async_computation.4 | async-start | bytes 4456448 | tf_op jit(solution)/shard_map/all_gather | solution.py:19
  1144.3 482.7 %all-gather.95.cloned.1.call-start = ((), (), s32[]{:S(2)}) async-start(), calls=%async_computation.23 | async-start | bytes 17825792 | tf_op jit(solution)/shard_map/all_gather | solution.py:19
  1516.0 224.6 %all-gather.93.cloned.1.call-start = ((), (), s32[]{:S(2)}) async-start(), calls=%async_computation.22 | async-start | bytes 17825792 | tf_op jit(solution)/shard_map/all_gather | solution.py:19
  1516.6 533.7 %all-gather.103.cloned.1.call-start = ((), (), s32[]{:S(2)}) async-start(), calls=%async_computation.27 | async-start | bytes 2359296 | tf_op jit(solution)/shard_map/all_gather | solution.py:19
  2022.7 111.1 %all-gather.97.cloned.1.call-start = ((), (), s32[]{:S(2)}) async-start(), calls=%async_computation.24 | async-start | bytes 2359296 | tf_op jit(solution)/shard_map/all_gather | solution.py:19
  2023.3 171.6 %all-gather.71.cloned.1.call-start = ((), (), s32[]{:S(2)}) async-start(), calls=%async_computation.11 | async-start | bytes 4456448 | tf_op jit(solution)/shard_map/all_gather | solution.py:19
  2142.9 105.1 %all-gather.69.cloned.1.call-start = ((), (), s32[]{:S(2)}) async-start(), calls=%async_computation.10 | async-start | bytes 4456448 | tf_op jit(solution)/shard_map/all_gather | solution.py:19
  2146.6 155.1 %all-gather.67.cloned.1.call-start = ((), (), s32[]{:S(2)}) async-start(), calls=%async_computation.9 | async-start | bytes 4456448 | tf_op jit(solution)/shard_map/all_gather | solution.py:19
  2150.2 204.7 %all-gather.65.cloned.1.call-start = ((), (), s32[]{:S(2)}) async-start(), calls=%async_computation.8 | async-start | bytes 4456448 | tf_op jit(solution)/shard_map/all_gather | solution.py:19
  2152.9 482.3 %all-gather.107.cloned.1.call-start = ((), (), s32[]{:S(2)}) async-start(), calls=%async_computation.29 | async-start | bytes 17825792 | tf_op jit(solution)/shard_map/all_gather | solution.py:19
  2524.2 224.6 %all-gather.105.cloned.1.call-start = ((), (), s32[]{:S(2)}) async-start(), calls=%async_computation.28 | async-start | bytes 17825792 | tf_op jit(solution)/shard_map/all_gather | solution.py:19
  (40 other events, 1102.3 us)
Sparse Core Ops, SparseCore 0:
  10.3 27.8 all-gather.78
  40.5 25.7 all-gather.76
  68.6 25.7 all-gather.74
  125.3 51.7 all-gather.54
  179.7 51.0 all-gather.52
  233.6 51.1 all-gather.50
  286.9 51.1 all-gather.48
  481.0 110.9 all-gather.82
  594.6 110.8 all-gather.80
  1012.6 28.6 all-gather.90
  1071.6 25.7 all-gather.86
  1134.5 51.7 all-gather.62
  1188.3 51.0 all-gather.60
  1242.0 51.1 all-gather.58
  1295.1 51.0 all-gather.56
  1516.1 110.8 all-gather.94
  1629.6 110.8 all-gather.92
  2021.3 28.9 all-gather.102
  2143.0 51.7 all-gather.70
  2196.8 51.0 all-gather.68
  2250.5 51.1 all-gather.66
  2303.8 51.1 all-gather.64
  2524.3 110.8 all-gather.106
  2637.8 110.8 all-gather.104
  (6 shorter events, 154.2 us)
